TPU v7x, 256 devices: a whole 4x4x8 slice. The times are simulated.
256 devices in a mesh: shard: 16 (over z, core), tensor: 4 (over x), section: 4 (over y).
Axes of the slice: x: 4, y: 4, z: 8, core: 2. Of those that a mesh axis runs over, the one named last changes fastest.
Arguments:
- gradient: bfloat16 [6, 2048, 8192], P(None, ('tensor', 'section'), 'shard'), may hold values from -6 to 6
- basis: bfloat16 [6, 2048, 256], P(None, ('tensor', 'section')), may hold values from -6 to 6
- moment_m: float32 [6, 8192, 256], P(None, ('shard', 'tensor', 'section')), may hold values from -4 to 4
- moment_v: float32 [6, 8192, 256], P(None, ('shard', 'tensor', 'section')), may hold values from 0.002 to 0.02
Outputs:
- delta: bfloat16 [6, 2048, 8192], P(None, ('tensor', 'section'), 'shard')
- basis_new: bfloat16 [6, 2048, 256], P(None, ('tensor', 'section'))
- moment_m_new: float32 [6, 8192, 256], P(None, ('shard', 'tensor', 'section'))
- moment_v_new: float32 [6, 8192, 256], P(None, ('shard', 'tensor', 'section'))
All inputs are finite; a program needn't handle non-finite values. Where the computation divides by a largest or mean magnitude, that divisor is 1e-20 or more.
Results may differ from a plain program's by a relative error of at most 0.0049.
Values may be sent and summed in bfloat16 or wider, within the bound.
A program may use at most 64 MiB of HBM per device.

v0:
```python
import math
import jax
import jax.numpy as jnp
from jax import lax
from jax.sharding import PartitionSpec as P

D = 2048
NS_ITERS = 4
beta_one = 0.9
beta_two = 0.999
bias_one = 1.0 - 0.9**10
bias_two = 1.0 - 0.999**10
eps_adam = 1e-08
galore_gain = 4.0


def gram_total(iterate):
    local_gram = jnp.einsum("kmr,kms->krs", iterate, iterate, precision=lax.Precision.HIGHEST)
    return lax.psum(local_gram, ("tensor", "section"))


def orthogonal(subspace):
    gram_mat = gram_total(subspace)
    row_bound = jnp.max(jnp.sum(jnp.abs(gram_mat), axis=2), axis=1)[:, None, None] + 1e-06
    iterate = subspace / jnp.sqrt(row_bound)
    gram_mat = gram_mat / row_bound
    identity = jnp.eye(gram_mat.shape[1], dtype=jnp.float32)
    for turn_index in range(NS_ITERS):
        factor = 1.5 * identity - 0.5 * gram_mat
        iterate = jnp.einsum("kmr,krs->kms", iterate, factor, precision=lax.Precision.HIGHEST)
        if turn_index + 1 < NS_ITERS:
            gram_mat = gram_total(iterate)
    return iterate


def per_device(gradient, basis, moment_m, moment_v):
    width_root = math.sqrt(D)
    partial_low = jnp.einsum("kmn,kmr->knr", gradient, basis, preferred_element_type=jnp.float32)
    low_rank = (
        lax.psum_scatter(partial_low, ("tensor", "section"), scatter_dimension=1, tiled=True)
        / width_root
    )
    moment_m_new = beta_one * moment_m + (1.0 - beta_one) * low_rank
    moment_v_new = beta_two * moment_v + (1.0 - beta_two) * low_rank * low_rank
    step_low = (moment_m_new / bias_one / (jnp.sqrt(moment_v_new / bias_two) + eps_adam)).astype(
        jnp.bfloat16
    )
    rough_low = low_rank.astype(jnp.bfloat16)
    step_block, rough_block = (
        lax.all_gather(step_low, ("tensor", "section"), axis=1, tiled=True),
        lax.all_gather(rough_low, ("tensor", "section"), axis=1, tiled=True),
    )
    delta = (
        -galore_gain
        / width_root
        * jnp.einsum("kmr,knr->kmn", basis, step_block, preferred_element_type=jnp.float32)
    ).astype(jnp.bfloat16)
    subspace = jnp.einsum("kmn,knr->kmr", gradient, rough_block, preferred_element_type=jnp.float32)
    whole_sum = lax.psum(subspace, "shard")
    basis_new = (width_root * orthogonal(whole_sum)).astype(jnp.bfloat16)
    return (delta, basis_new, moment_m_new, moment_v_new)


def solution(mesh):
    placed = (
        P(None, ("tensor", "section"), "shard"),
        P(None, ("tensor", "section"), None),
        P(None, ("shard", "tensor", "section"), None),
        P(None, ("shard", "tensor", "section"), None),
    )
    return jax.shard_map(
        per_device,
        mesh=mesh,
        in_specs=placed,
        out_specs=(
            P(None, ("tensor", "section"), "shard"),
            P(None, ("tensor", "section"), None),
            P(None, ("shard", "tensor", "section"), None),
            P(None, ("shard", "tensor", "section"), None),
        ),
        check_vma=False,
    )
```

profile of v0, /device:TPU:32, one launch (start us, length us, event | category | flops | bytes accessed | tf_op | source)
XLA Modules:
  0.0 738.4 jit_solution(1374766177256162602)
XLA Ops:
  7.2 0.0 copy-start
  7.2 0.0 reduce-scatter.2.cloned.1.call-start
  7.2 1.1 copy-done
  8.3 3.3 fusion.37
  11.6 0.0 copy-start.3
  11.6 0.0 copy-start.4
  11.6 0.0 reduce-scatter.2.cloned.1.call-update
  11.6 0.0 all-gather.5.cloned.1.call-start
  11.6 84.4 %reduce-scatter.2.cloned.1.call-done = f32[6,32,256]{2,1,0:T(8,128)} async-done(((f32[6,512,256]{2,1,0:T(8,128)}), f32[6,32,256]{2,1,0:T(8,128)}) %reduce-scatter.2.cloned.1.call-update) | async-done | bytes 196624 | tf_op jit(solution)/shard_map/reduce_scatter | solution.py:40
  96.0 0.0 copy-done.3
  96.0 0.0 copy-done.4
  96.0 1.8 divide_convert_fusion
  97.8 0.0 all-gather.5.cloned.1.call-update
  97.9 0.0 all-reduce.6.cloned.1.call-start
  97.9 49.2 %all-gather.5.cloned.1.call-done = bf16[6,512,256]{2,1,0:T(8,128)(2,1)} async-done(((bf16[6,32,256]{2,1,0:T(8,128)(2,1)}), bf16[6,512,256]{2,1,0:T(8,128)(2,1)}) %all-gather.5.cloned.1.call-update) | async-done | bytes 1572880 | tf_op jit(solution)/shard_map/all_gather | solution.py:51
  147.2 2.9 convolution_bitcast_fusion
  150.1 0.0 all-reduce.6.cloned.1.call-update
  150.1 0.0 all-reduce.8.cloned.1.call-start
  150.2 108.3 %all-reduce.6.cloned.1.call-done = f32[6,128,256]{1,2,0:T(8,128)} async-done(((f32[6,128,256]{1,2,0:T(8,128)}), f32[6,128,256]{1,2,0:T(8,128)}) %all-reduce.6.cloned.1.call-update) | async-done | bytes 786448 | tf_op jit(solution)/shard_map/psum | solution.py:59
  258.5 3.9 fusion.38
  262.4 0.0 copy-start.1
  262.4 0.0 all-reduce.8.cloned.1.call-update
  262.5 0.0 all-reduce.10.cloned.1.call-start
  262.5 102.3 %all-reduce.8.cloned.1.call-done = f32[6,256,256]{2,1,0:T(8,128)} async-done(((f32[6,256,256]{2,1,0:T(8,128)}), f32[6,256,256]{2,1,0:T(8,128)}) %all-reduce.8.cloned.1.call-update) | async-done | bytes 1572880 | tf_op jit(solution)/shard_map/psum | solution.py:19
  364.8 1.7 abs_reduce_fusion
  366.5 0.1 reduce_max.9
  366.6 0.0 copy-done.1
  366.6 3.2 fusion.9
  369.8 2.6 fusion.39
  372.4 0.0 all-reduce.10.cloned.1.call-update
  372.4 0.0 all-reduce.12.cloned.1.call-start
  372.5 98.7 %all-reduce.10.cloned.1.call-done = f32[6,256,256]{2,1,0:T(8,128)} async-done(((f32[6,256,256]{2,1,0:T(8,128)}), f32[6,256,256]{2,1,0:T(8,128)}) %all-reduce.10.cloned.1.call-update) | async-done | bytes 1572880 | tf_op jit(solution)/shard_map/psum | solution.py:19
  471.1 2.6 fusion.6
  473.7 2.6 fusion.40
  476.3 0.0 all-reduce.12.cloned.1.call-update
  476.4 0.0 all-gather.3.cloned.1.call-start
  476.4 0.7 all-gather.3.cloned.1.call-update
  477.1 0.2 all-reduce.14.cloned.1.call-start
  477.3 97.7 %all-reduce.12.cloned.1.call-done = f32[6,256,256]{2,1,0:T(8,128)} async-done(((f32[6,256,256]{2,1,0:T(8,128)}), f32[6,256,256]{2,1,0:T(8,128)}) %all-reduce.12.cloned.1.call-update) | async-done | bytes 1572880 | tf_op jit(solution)/shard_map/psum | solution.py:19
  575.1 2.6 fusion.3
  577.6 2.6 fusion.41
  580.3 0.0 copy-start.2
  580.3 0.0 all-reduce.14.cloned.1.call-update
  580.3 46.1 %all-gather.3.cloned.1.call-done = bf16[6,512,256]{2,1,0:T(8,128)(2,1)} async-done(((bf16[6,32,256]{2,1,0:T(8,128)(2,1)}), bf16[6,512,256]{2,1,0:T(8,128)(2,1)}) %all-gather.3.cloned.1.call-update) | async-done | bytes 1572880 | tf_op jit(solution)/shard_map/all_gather | solution.py:50
  626.4 0.0 copy-done.2
  626.4 2.0 fusion.13
  628.3 1.2 copy.15
  629.5 98.7 %all-reduce.14.cloned.1.call-done = f32[6,256,256]{2,1,0:T(8,128)} async-done(((f32[6,256,256]{2,1,0:T(8,128)}), f32[6,256,256]{2,1,0:T(8,128)}) %all-reduce.14.cloned.1.call-update) | async-done | bytes 1572880 | tf_op jit(solution)/shard_map/psum | solution.py:19
  728.2 3.3 fusion.17
  (2 shorter events, 0.0 us)
Async XLA Ops:
  7.2 1.1 copy-start
  7.2 88.8 %reduce-scatter.2.cloned.1.call-start = ((), (), s32[]{:S(2)}) async-start(), calls=%async_computation.1 | async-start | bytes 3342336 | tf_op jit(solution)/shard_map/reduce_scatter | solution.py:40
  11.6 84.4 %copy-start.3 = (f32[6,32,256]{2,1,0:T(8,128)S(1)}, f32[6,32,256]{2,1,0:T(8,128)}, u32[]{:S(2)}) copy-start(f32[6,32,256]{2,1,0:T(8,128)} %param.6) | copy-start | bytes 589828
  11.6 84.4 %copy-start.4 = (f32[6,32,256]{2,1,0:T(8,128)S(1)}, f32[6,32,256]{2,1,0:T(8,128)}, u32[]{:S(2)}) copy-start(f32[6,32,256]{2,1,0:T(8,128)} %param.7) | copy-start | bytes 589828
  11.6 135.6 %all-gather.5.cloned.1.call-start = ((), (), s32[]{:S(2)}) async-start(), calls=%async_computation.3 | async-start | bytes 1671168 | tf_op jit(solution)/shard_map/all_gather | solution.py:51
  97.9 160.6 %all-reduce.6.cloned.1.call-start = ((), (), s32[]{:S(2)}) async-start(), calls=%async_computation.4 | async-start | bytes 1572864 | tf_op jit(solution)/shard_map/psum | solution.py:59
  150.1 214.7 %all-reduce.8.cloned.1.call-start = ((), (), s32[]{:S(2)}) async-start(), calls=%async_computation.5 | async-start | bytes 3145728 | tf_op jit(solution)/shard_map/psum | solution.py:19
  262.4 104.2 %copy-start.1 = (f32[6,128,256]{1,2,0:T(8,128)S(1)}, f32[6,128,256]{1,2,0:T(8,128)}, u32[]{:S(2)}) copy-start(f32[6,128,256]{1,2,0:T(8,128)} %all-reduce.6.cloned.1.call-done) | copy-start | bytes 2359300
  262.5 208.7 %all-reduce.10.cloned.1.call-start = ((), (), s32[]{:S(2)}) async-start(), calls=%async_computation.6 | async-start | bytes 3145728 | tf_op jit(solution)/shard_map/psum | solution.py:19
  372.4 202.6 %all-reduce.12.cloned.1.call-start = ((), (), s32[]{:S(2)}) async-start(), calls=%async_computation.7 | async-start | bytes 3145728 | tf_op jit(solution)/shard_map/psum | solution.py:19
  476.4 150.0 %all-gather.3.cloned.1.call-start = ((), (), s32[]{:S(2)}) async-start(), calls=%async_computation.2 | async-start | bytes 1671168 | tf_op jit(solution)/shard_map/all_gather | solution.py:50
  477.1 251.1 %all-reduce.14.cloned.1.call-start = ((), (), s32[]{:S(2)}) async-start(), calls=%async_computation.8 | async-start | bytes 3145728 | tf_op jit(solution)/shard_map/psum | solution.py:19
  580.3 46.1 %copy-start.2 = (bf16[6,128,256]{2,1,0:T(8,128)(2,1)S(1)}, bf16[6,128,256]{2,1,0:T(8,128)(2,1)}, u32[]{:S(2)}) copy-start(bf16[6,128,256]{2,1,0:T(8,128)(2,1)} %param.5) | copy-start | bytes 1179652
Sparse Core Ops, SparseCore 0:
  11.7 84.2 reduce-scatter.1
  99.1 48.0 all-gather.4
  150.2 108.2 all-reduce.5
  262.6 102.1 all-reduce.7
  372.6 98.5 all-reduce.9
  476.5 98.5 all-reduce.11
  578.1 48.1 all-gather.2
  629.7 98.5 all-reduce.13
where the time goes:
time: 739 us; the launch traced here: 738 us
  waiting for transfers between devices  686 us (93%)
  matrix products  31.6 us (4%)
  between operations  14.2 us (2%)
    psum x4, waiting for transfers between devices, gram_total(): return lax.psum(local_gram, ('tensor', 'section'))  397 us
    psum x1, waiting for transfers between devices, per_device(): whole_sum = lax.psum(subspace, 'shard')  108 us
    reduce_scatter x1, waiting for transfers between devices, per_device(): lax.psum_scatter(partial_low, ('tensor', 'section'), scatter_dimension=1,...  84.4 us
    all_gather x1, waiting for transfers between devices, per_device(): lax.all_gather(rough_low, ('tensor', 'section'), axis=1, tiled=True)  49.2 us
    all_gather x1, waiting for transfers between devices, per_device(): lax.all_gather(step_low, ('tensor', 'section'), axis=1, tiled=True)  46.1 us
  transfers between devices with their start and end apart: 8, of which 8 were waited for; matrix products, arithmetic and copies ran while one was open for 1% of the time, Pallas kernels for 0%

commit v1 on v0

--- a/solution.py
+++ b/solution.py
@@ -56,7 +56,11 @@
         * jnp.einsum("kmr,knr->kmn", basis, step_block, preferred_element_type=jnp.float32)
     ).astype(jnp.bfloat16)
     subspace = jnp.einsum("kmn,knr->kmr", gradient, rough_block, preferred_element_type=jnp.float32)
-    whole_sum = lax.psum(subspace, "shard")
+    whole_sum = subspace
+    for hop in (1, 2, 4, 8):
+        whole_sum = whole_sum + lax.ppermute(
+            whole_sum, "shard", [(dev, dev ^ hop) for dev in range(16)]
+        )
     basis_new = (width_root * orthogonal(whole_sum)).astype(jnp.bfloat16)
     return (delta, basis_new, moment_m_new, moment_v_new)
 

time: 739 us -> 721 us (0.976)
  waiting for transfers between devices: 686 us -> 664 us
    psum x1 -> x0, waiting for transfers between devices: 108 us -> none  [per_device(): whole_sum = lax.psum(subspace, 'shard')]
    ppermute x0 -> x4, waiting for transfers between devices: none -> 75.6 us  [per_device(): lax.ppermute(whole_sum, 'shard', [(dev, dev ^ hop) for dev in range(16)])]
    psum x4, waiting for transfers between devices: 397 us -> 408 us  [gram_total(): return lax.psum(local_gram, ('tensor', 'section'))]
  transfers between devices with their start and end apart: 8 -> 11, of which waited for: 8 -> 11; matrix products, arithmetic and copies ran while one was open for 1% -> 1% of each run, Pallas kernels for 0% -> 0%
where the time goes in v1:
time: 721 us
  waiting for transfers between devices  664 us (92%)
  matrix products  29.3 us (4%)
  between operations  14.2 us (2%)
    psum x4, waiting for transfers between devices, gram_total(): return lax.psum(local_gram, ('tensor', 'section'))  408 us
    reduce_scatter x1, waiting for transfers between devices, per_device(): lax.psum_scatter(partial_low, ('tensor', 'section'), scatter_dimension=1,...  84.3 us
    ppermute x4, waiting for transfers between devices, per_device(): lax.ppermute(whole_sum, 'shard', [(dev, dev ^ hop) for dev in range(16)])  75.6 us
    all_gather x1, waiting for transfers between devices, per_device(): lax.all_gather(rough_low, ('tensor', 'section'), axis=1, tiled=True)  49.2 us
    all_gather x1, waiting for transfers between devices, per_device(): lax.all_gather(step_low, ('tensor', 'section'), axis=1, tiled=True)  45.9 us
  transfers between devices with their start and end apart: 11, of which 11 were waited for; matrix products, arithmetic and copies ran while one was open for 1% of the time, Pallas kernels for 0%

profile of v1, /device:TPU:32, one launch (start us, length us, event | category | flops | bytes accessed | tf_op | source)
XLA Modules:
  0.0 720.6 jit_solution(1530033249101446691)
XLA Ops:
  7.2 0.0 copy-start
  7.2 0.0 reduce-scatter.2.cloned.1.call-start
  7.2 1.1 copy-done
  8.3 3.2 fusion.37
  11.6 0.0 copy-start.2
  11.6 0.0 copy-start.3
  11.6 0.0 reduce-scatter.2.cloned.1.call-update
  11.6 0.0 all-gather.5.cloned.1.call-start
  11.6 84.3 %reduce-scatter.2.cloned.1.call-done = f32[6,32,256]{2,1,0:T(8,128)} async-done(((f32[6,512,256]{2,1,0:T(8,128)}), f32[6,32,256]{2,1,0:T(8,128)}) %reduce-scatter.2.cloned.1.call-update) | async-done | bytes 196624 | tf_op jit(solution)/shard_map/reduce_scatter | solution.py:40
  96.0 0.0 copy-done.2
  96.0 0.0 copy-done.3
  96.0 1.8 divide_convert_fusion
  97.8 0.0 all-gather.5.cloned.1.call-update
  97.8 0.0 all-reduce.5.cloned.1.call-start
  97.9 49.2 %all-gather.5.cloned.1.call-done = bf16[6,512,256]{2,1,0:T(8,128)(2,1)} async-done(((bf16[6,32,256]{2,1,0:T(8,128)(2,1)}), bf16[6,512,256]{2,1,0:T(8,128)(2,1)}) %all-gather.5.cloned.1.call-update) | async-done | bytes 1572880 | tf_op jit(solution)/shard_map/all_gather | solution.py:51
  147.1 2.1 convolution_bitcast_fusion
  149.2 0.1 collective-permute-start
  149.3 2.3 collective-permute-done
  151.5 0.1 add.49
  151.7 0.6 collective-permute-start.1
  152.2 19.1 %collective-permute-done.1 = f32[6,128,256]{1,2,0:T(8,128)S(1)} collective-permute-done((f32[6,128,256]{1,2,0:T(8,128)S(1)}, f32[6,128,256]{1,2,0:T(8,128)S(1)}, u32[]{:S(2)}, u32[]{:S(2)}) %collective-permute-start.1) | collective-permute-done | bytes 786464 | tf_op jit(solution)/shard_map/ppermute | solution.py:61
  171.3 0.1 add.50
  171.4 2.6 collective-permute-start.2
  174.1 33.0 %collective-permute-done.2 = f32[6,128,256]{1,2,0:T(8,128)S(1)} collective-permute-done((f32[6,128,256]{1,2,0:T(8,128)S(1)}, f32[6,128,256]{1,2,0:T(8,128)S(1)}, u32[]{:S(2)}, u32[]{:S(2)}) %collective-permute-start.2) | collective-permute-done | bytes 786464 | tf_op jit(solution)/shard_map/ppermute | solution.py:61
  207.1 0.1 add.51
  207.1 3.2 collective-permute-start.3
  210.4 21.2 %collective-permute-done.3 = f32[6,128,256]{1,2,0:T(8,128)S(1)} collective-permute-done((f32[6,128,256]{1,2,0:T(8,128)S(1)}, f32[6,128,256]{1,2,0:T(8,128)S(1)}, u32[]{:S(2)}, u32[]{:S(2)}) %collective-permute-start.3) | collective-permute-done | bytes 786464 | tf_op jit(solution)/shard_map/ppermute | solution.py:61
  231.6 0.1 add.52
  231.7 2.6 fusion.38
  234.2 0.0 all-reduce.5.cloned.1.call-update
  234.2 0.0 all-reduce.7.cloned.1.call-start
  234.3 112.8 %all-reduce.5.cloned.1.call-done = f32[6,256,256]{2,1,0:T(8,128)} async-done(((f32[6,256,256]{2,1,0:T(8,128)}), f32[6,256,256]{2,1,0:T(8,128)}) %all-reduce.5.cloned.1.call-update) | async-done | bytes 1572880 | tf_op jit(solution)/shard_map/psum | solution.py:19
  347.1 1.7 abs_reduce_fusion
  348.8 0.1 reduce_max.9
  348.9 3.2 fusion.9
  352.1 2.6 fusion.39
  354.7 0.0 all-reduce.7.cloned.1.call-update
  354.7 0.2 all-reduce.9.cloned.1.call-start
  355.0 98.5 %all-reduce.7.cloned.1.call-done = f32[6,256,256]{2,1,0:T(8,128)} async-done(((f32[6,256,256]{2,1,0:T(8,128)}), f32[6,256,256]{2,1,0:T(8,128)}) %all-reduce.7.cloned.1.call-update) | async-done | bytes 1572880 | tf_op jit(solution)/shard_map/psum | solution.py:19
  453.4 2.6 fusion.6
  456.0 2.6 fusion.40
  458.6 0.0 all-reduce.9.cloned.1.call-update
  458.7 0.0 all-gather.3.cloned.1.call-start
  458.7 0.5 all-gather.3.cloned.1.call-update
  459.2 0.0 all-reduce.11.cloned.1.call-start
  459.3 98.1 %all-reduce.9.cloned.1.call-done = f32[6,256,256]{2,1,0:T(8,128)} async-done(((f32[6,256,256]{2,1,0:T(8,128)}), f32[6,256,256]{2,1,0:T(8,128)}) %all-reduce.9.cloned.1.call-update) | async-done | bytes 1572880 | tf_op jit(solution)/shard_map/psum | solution.py:19
  557.4 2.6 fusion.3
  559.9 2.6 fusion.41
  562.6 0.0 copy-start.1
  562.6 0.0 all-reduce.11.cloned.1.call-update
  562.6 45.9 %all-gather.3.cloned.1.call-done = bf16[6,512,256]{2,1,0:T(8,128)(2,1)} async-done(((bf16[6,32,256]{2,1,0:T(8,128)(2,1)}), bf16[6,512,256]{2,1,0:T(8,128)(2,1)}) %all-gather.3.cloned.1.call-update) | async-done | bytes 1572880 | tf_op jit(solution)/shard_map/all_gather | solution.py:50
  608.5 0.0 copy-done.1
  608.5 2.0 fusion.13
  610.5 1.2 copy.15
  611.7 98.7 %all-reduce.11.cloned.1.call-done = f32[6,256,256]{2,1,0:T(8,128)} async-done(((f32[6,256,256]{2,1,0:T(8,128)}), f32[6,256,256]{2,1,0:T(8,128)}) %all-reduce.11.cloned.1.call-update) | async-done | bytes 1572880 | tf_op jit(solution)/shard_map/psum | solution.py:19
  710.4 3.3 fusion.17
  (2 shorter events, 0.0 us)
Async XLA Ops:
  7.2 1.1 copy-start
  7.2 88.8 %reduce-scatter.2.cloned.1.call-start = ((), (), s32[]{:S(2)}) async-start(), calls=%async_computation.1 | async-start | bytes 3342336 | tf_op jit(solution)/shard_map/reduce_scatter | solution.py:40
  11.6 84.4 %copy-start.2 = (f32[6,32,256]{2,1,0:T(8,128)S(1)}, f32[6,32,256]{2,1,0:T(8,128)}, u32[]{:S(2)}) copy-start(f32[6,32,256]{2,1,0:T(8,128)} %param.6) | copy-start | bytes 589828
  11.6 84.4 %copy-start.3 = (f32[6,32,256]{2,1,0:T(8,128)S(1)}, f32[6,32,256]{2,1,0:T(8,128)}, u32[]{:S(2)}) copy-start(f32[6,32,256]{2,1,0:T(8,128)} %param.7) | copy-start | bytes 589828
  11.6 135.5 %all-gather.5.cloned.1.call-start = ((), (), s32[]{:S(2)}) async-start(), calls=%async_computation.3 | async-start | bytes 1671168 | tf_op jit(solution)/shard_map/all_gather | solution.py:51
  97.8 249.3 %all-reduce.5.cloned.1.call-start = ((), (), s32[]{:S(2)}) async-start(), calls=%async_computation.4 | async-start | bytes 3145728 | tf_op jit(solution)/shard_map/psum | solution.py:19
  149.2 2.4 collective-permute-start
  151.7 19.7 %collective-permute-start.1 = (f32[6,128,256]{1,2,0:T(8,128)S(1)}, f32[6,128,256]{1,2,0:T(8,128)S(1)}, u32[]{:S(2)}, u32[]{:S(2)}) collective-permute-start(f32[6,128,256]{1,2,0:T(8,128)S(1)} %add.49), channel_id=1, source_target_pairs={{0,32},{16,48},{32,0},{48,16},{64,96},{80,112},{96,64},{112,80},{1... | collective-permute-start | bytes 2359304 | tf_op jit(solution)/shard_map/ppermute | solution.py:61
  171.4 35.6 %collective-permute-start.2 = (f32[6,128,256]{1,2,0:T(8,128)S(1)}, f32[6,128,256]{1,2,0:T(8,128)S(1)}, u32[]{:S(2)}, u32[]{:S(2)}) collective-permute-start(f32[6,128,256]{1,2,0:T(8,128)S(1)} %add.50), channel_id=1, source_target_pairs={{0,64},{16,80},{32,96},{48,112},{64,0},{80,16},{96,32},{112,48},{1... | collective-permute-start | bytes 2359304 | tf_op jit(solution)/shard_map/ppermute | solution.py:61
  207.1 24.4 %collective-permute-start.3 = (f32[6,128,256]{1,2,0:T(8,128)S(1)}, f32[6,128,256]{1,2,0:T(8,128)S(1)}, u32[]{:S(2)}, u32[]{:S(2)}) collective-permute-start(f32[6,128,256]{1,2,0:T(8,128)S(1)} %add.51), channel_id=1, source_target_pairs={{0,128},{16,144},{32,160},{48,176},{64,192},{80,208},{96,224},{112... | collective-permute-start | bytes 2359304 | tf_op jit(solution)/shard_map/ppermute | solution.py:61
  234.2 219.2 %all-reduce.7.cloned.1.call-start = ((), (), s32[]{:S(2)}) async-start(), calls=%async_computation.5 | async-start | bytes 3145728 | tf_op jit(solution)/shard_map/psum | solution.py:19
  354.7 202.6 %all-reduce.9.cloned.1.call-start = ((), (), s32[]{:S(2)}) async-start(), calls=%async_computation.6 | async-start | bytes 3145728 | tf_op jit(solution)/shard_map/psum | solution.py:19
  458.7 149.8 %all-gather.3.cloned.1.call-start = ((), (), s32[]{:S(2)}) async-start(), calls=%async_computation.2 | async-start | bytes 1671168 | tf_op jit(solution)/shard_map/all_gather | solution.py:50
  459.2 251.2 %all-reduce.11.cloned.1.call-start = ((), (), s32[]{:S(2)}) async-start(), calls=%async_computation.7 | async-start | bytes 3145728 | tf_op jit(solution)/shard_map/psum | solution.py:19
  562.6 45.9 %copy-start.1 = (bf16[6,128,256]{2,1,0:T(8,128)(2,1)S(1)}, bf16[6,128,256]{2,1,0:T(8,128)(2,1)}, u32[]{:S(2)}) copy-start(bf16[6,128,256]{2,1,0:T(8,128)(2,1)} %param.5) | copy-start | bytes 1179652
Sparse Core Ops, SparseCore 0:
  11.7 84.2 reduce-scatter.1
  99.0 48.0 all-gather.4
  234.4 112.6 all-reduce.4
  354.9 98.5 all-reduce.6
  458.8 98.5 all-reduce.8
  560.3 48.1 all-gather.2
  611.8 98.5 all-reduce.10
